TPU v7x, 32 devices: a whole 2x2x4 slice. The times are simulated.
32 devices in a mesh: batch: 8 (over y, x, core), rows: 4 (over z).
Axes of the slice: x: 2, y: 2, z: 4, core: 2. Of those that a mesh axis runs over, the one named last changes fastest.
Arguments:
- atoms: bfloat16 [32, 256, 512], P('batch', 'rows'), may hold values from -6 to 6
- pair_bias: bfloat16 [32, 64, 256, 256], P('batch', None, 'rows'), may hold values from -6 to 6
- lengths: int32 [32], P('batch'), may hold values from 64 to 256, as said below
- first_gain: bfloat16 [512], replicated, may hold values from 0.099609375 to 1.8984375
- first_shift: bfloat16 [512], replicated, may hold values from -3 to 3
- query_weight: bfloat16 [512, 512], replicated, may hold values from -0.25 to 0.25
- query_bias: bfloat16 [512], replicated, may hold values from -3 to 3
- key_weight: bfloat16 [512, 512], replicated, may hold values from -0.25 to 0.25
- value_weight: bfloat16 [512, 512], replicated, may hold values from -0.25 to 0.25
- value_bias: bfloat16 [512], replicated, may hold values from -3 to 3
- out_weight: bfloat16 [512, 512], replicated, may hold values from -1 to 1
- out_bias: bfloat16 [512], replicated, may hold values from -3 to 3
- second_gain: bfloat16 [512], replicated, may hold values from 0.099609375 to 1.8984375
- second_shift: bfloat16 [512], replicated, may hold values from -3 to 3
- inner_weight: bfloat16 [512, 2048], replicated, may hold values from -0.25 to 0.25
- inner_bias: bfloat16 [2048], replicated, may hold values from -3 to 3
- outer_weight: bfloat16 [2048, 512], replicated, may hold values from -0.125 to 0.125
- outer_bias: bfloat16 [512], replicated, may hold values from -3 to 3
- atoms_cotangent: bfloat16 [32, 256, 512], P('batch', 'rows'), may hold values from -6 to 6
- pair_cotangent: bfloat16 [32, 64, 256, 256], P('batch', None, 'rows'), may hold values from -6 to 6
Outputs:
- atoms_out: bfloat16 [32, 256, 512], P('batch', 'rows')
- pair_out: bfloat16 [32, 64, 256, 256], P('batch', None, 'rows')
- atoms_grad: bfloat16 [32, 256, 512], P('batch', 'rows')
- pair_grad: bfloat16 [32, 64, 256, 256], P('batch', None, 'rows')
- first_gain_grad: float32 [512], P('batch')
- first_shift_grad: float32 [512], P('batch')
- query_weight_grad: float32 [512, 512], P('batch')
- query_bias_grad: float32 [512], P('batch')
- key_weight_grad: float32 [512, 512], P('batch')
- value_weight_grad: float32 [512, 512], P('batch')
- value_bias_grad: float32 [512], P('batch')
- out_weight_grad: float32 [512, 512], P('batch')
- out_bias_grad: float32 [512], P('batch')
- second_gain_grad: float32 [512], P('batch')
- second_shift_grad: float32 [512], P('batch')
- inner_weight_grad: float32 [512, 2048], P('batch')
- inner_bias_grad: float32 [2048], P('batch')
- outer_weight_grad: float32 [2048, 512], P('batch')
- outer_bias_grad: float32 [512], P('batch')
Inputs may be any that keep to these rules, and one draw needn't show every extreme that they name: Atoms at positions lengths[m] and beyond are padding and are masked as keys; of the 4 molecules at each index of batch, one (drawn from the seed) has exactly 256 atoms.
All inputs are finite; a program needn't handle non-finite values.
Results may differ from a plain program's by a relative error of at most 0.012.
Values may be sent and summed in bfloat16 or wider, within the bound.
No kernel may reach another device: no remote copies, remote signals or barrier semaphores. Data moves between devices by JAX's collectives and lax.ppermute only.
A program may use at most 128 MiB of HBM per device.

v0:
```python
from functools import partial
import jax
import jax.numpy as jnp
from jax import lax
from jax.sharding import PartitionSpec as P

EPSILON = 1e-05
MASKED = -1000000000.0


def norm_forward(values_in, gain, shift):
    centre = values_in - jnp.mean(values_in, -1, keepdims=True)
    inverse = lax.rsqrt(jnp.mean(centre * centre, -1, keepdims=True) + EPSILON)
    normed = centre * inverse
    return (normed * gain + shift, normed, inverse)


def norm_backward(upstream, normed, inverse, gain):
    scaled = upstream * gain
    result = inverse * (
        scaled
        - jnp.mean(scaled, -1, keepdims=True)
        - normed * jnp.mean(scaled * normed, -1, keepdims=True)
    )
    return (result, jnp.sum(upstream * normed, 0), jnp.sum(upstream, 0))


def across(left, right):
    return lax.dot_general(
        left, right, (((0,), (0,)), ((), ())), preferred_element_type=jnp.float32
    )


def against(left, right):
    return lax.dot_general(
        left, right, (((1,), (1,)), ((), ())), preferred_element_type=jnp.float32
    )


def column_sum(values_in):
    return jnp.sum(values_in.astype(jnp.float32), 0)


def project_keys(hidden_rows, key_weight, value_weight, value_bias):
    key_rows = jnp.dot(hidden_rows, key_weight, preferred_element_type=jnp.float32).astype(
        jnp.bfloat16
    )
    value_rows = (
        jnp.dot(hidden_rows, value_weight, preferred_element_type=jnp.float32)
        + value_bias.astype(jnp.float32)
    ).astype(jnp.bfloat16)
    return (key_rows, value_rows)


def scores_of(factor, query_rows, key_rows, pair_rows, length):
    scores = factor * jnp.einsum(
        "ihe,jhe->hij", query_rows, key_rows, preferred_element_type=jnp.float32
    )
    scores = scores + pair_rows.astype(jnp.float32)
    valid = lax.broadcasted_iota(jnp.int32, scores.shape, 2) < length
    return (scores, valid)


def attend_forward(factor, pieces):
    query_rows, key_rows, value_rows, pair_rows, length = pieces
    scores, valid = scores_of(factor, query_rows, key_rows, pair_rows, length)
    masked = jnp.where(valid, scores, MASKED)
    highest = jnp.max(masked, -1, keepdims=True)
    weights = jnp.exp(masked - highest)
    totals = jnp.sum(weights, -1, keepdims=True)
    low_probs = (weights / totals).astype(jnp.bfloat16)
    mixed_rows = jnp.einsum(
        "hij,jhe->ihe", low_probs, value_rows, preferred_element_type=jnp.float32
    )
    return (
        scores.astype(jnp.bfloat16),
        mixed_rows.astype(jnp.bfloat16),
        (highest + jnp.log(totals))[..., 0],
    )


def attend_backward(factor, pieces):
    query_rows, key_rows, value_rows, pair_rows, length, log_totals, mixed_grad, pair_cot = pieces
    scores, valid = scores_of(factor, query_rows, key_rows, pair_rows, length)
    probs = jnp.exp(jnp.where(valid, scores, MASKED) - log_totals[..., None])
    low_probs = probs.astype(jnp.bfloat16)
    probs_grad = jnp.einsum(
        "ihe,jhe->hij", mixed_grad, value_rows, preferred_element_type=jnp.float32
    )
    value_grad = jnp.einsum(
        "hij,ihe->jhe", low_probs, mixed_grad, preferred_element_type=jnp.float32
    )
    inner_sum = jnp.sum(probs * probs_grad, -1, keepdims=True)
    score_grad = (probs * (probs_grad - inner_sum) + pair_cot.astype(jnp.float32)).astype(
        jnp.bfloat16
    )
    query_grad = factor * jnp.einsum(
        "hij,jhe->ihe", score_grad, key_rows, preferred_element_type=jnp.float32
    )
    key_grad = factor * jnp.einsum(
        "hij,ihe->jhe", score_grad, query_rows, preferred_element_type=jnp.float32
    )
    return (score_grad, query_grad.astype(jnp.bfloat16), key_grad, value_grad)


def shards(
    atoms,
    pair_bias,
    lengths,
    first_gain,
    first_shift,
    query_weight,
    query_bias,
    key_weight,
    value_weight,
    value_bias,
    out_weight,
    out_bias,
    second_gain,
    second_shift,
    inner_weight,
    inner_bias,
    outer_weight,
    outer_bias,
    atoms_cotangent,
    pair_cotangent,
):
    floats = jnp.float32
    halves = jnp.bfloat16
    molecules, atom_rows, model_width = atoms.shape
    head_count = pair_bias.shape[1]
    head_size = model_width // head_count
    factor = head_size ** (-0.5)
    tokens = molecules * atom_rows
    atoms_float = atoms.astype(floats).reshape(tokens, model_width)
    first_out, first_normed, first_inverse = norm_forward(
        atoms_float, first_gain.astype(floats), first_shift.astype(floats)
    )
    first_low = first_out.astype(halves)
    query_low = (
        jnp.dot(first_low, query_weight, preferred_element_type=floats) + query_bias.astype(floats)
    ).astype(halves)
    first_grouped = first_low.reshape(molecules, atom_rows, model_width)
    key_local, value_local = project_keys(first_grouped, key_weight, value_weight, value_bias)
    all_keys, all_values = (
        lax.all_gather(key_local, "rows", axis=1, tiled=True),
        lax.all_gather(value_local, "rows", axis=1, tiled=True),
    )
    key_count = all_keys.shape[1]
    query_heads = query_low.reshape(molecules, atom_rows, head_count, head_size)
    key_heads = all_keys.reshape(molecules, key_count, head_count, head_size)
    value_heads = all_values.reshape(molecules, key_count, head_count, head_size)
    pair_out, mixed_heads, log_totals = lax.map(
        partial(attend_forward, factor), (query_heads, key_heads, value_heads, pair_bias, lengths)
    )
    mixed_low = mixed_heads.reshape(tokens, model_width)
    middle = (
        atoms_float
        + jnp.dot(mixed_low, out_weight, preferred_element_type=floats)
        + out_bias.astype(floats)
    )
    second_out, second_normed, second_inverse = norm_forward(
        middle, second_gain.astype(floats), second_shift.astype(floats)
    )
    second_low = second_out.astype(halves)
    inner_pre = jnp.dot(
        second_low, inner_weight, preferred_element_type=floats
    ) + inner_bias.astype(floats)
    activated, gelu_pull = jax.vjp(jax.nn.gelu, inner_pre)
    activated_low = activated.astype(halves)
    result_rows = (
        middle
        + jnp.dot(activated_low, outer_weight, preferred_element_type=floats)
        + outer_bias.astype(floats)
    )
    atoms_out = result_rows.astype(halves).reshape(molecules, atom_rows, model_width)
    grad_outer = atoms_cotangent.reshape(tokens, model_width)
    outer_weight_grad = across(activated_low, grad_outer)
    outer_bias_grad = column_sum(grad_outer)
    grad_activated = against(grad_outer, outer_weight)
    grad_inner = gelu_pull(grad_activated)[0].astype(halves)
    inner_weight_grad = across(second_low, grad_inner)
    inner_bias_grad = column_sum(grad_inner)
    grad_second = against(grad_inner, inner_weight)
    second_back, second_gain_grad, second_shift_grad = norm_backward(
        grad_second, second_normed, second_inverse, second_gain.astype(floats)
    )
    grad_middle = grad_outer.astype(floats) + second_back
    grad_branch = grad_middle.astype(halves)
    out_weight_grad = across(mixed_low, grad_branch)
    out_bias_grad = column_sum(grad_branch)
    grad_mixed = against(grad_branch, out_weight).astype(halves)
    pair_grad, query_grad, key_grad, value_grad = lax.map(
        partial(attend_backward, factor),
        (
            query_heads,
            key_heads,
            value_heads,
            pair_bias,
            lengths,
            log_totals,
            grad_mixed.reshape(molecules, atom_rows, head_count, head_size),
            pair_cotangent,
        ),
    )
    key_share, value_share = (
        lax.psum_scatter(
            key_grad.reshape(molecules, key_count, model_width),
            "rows",
            scatter_dimension=1,
            tiled=True,
        ),
        lax.psum_scatter(
            value_grad.reshape(molecules, key_count, model_width),
            "rows",
            scatter_dimension=1,
            tiled=True,
        ),
    )
    key_grad_low = key_share.reshape(tokens, model_width).astype(halves)
    value_grad_low = value_share.reshape(tokens, model_width).astype(halves)
    query_grad_low = query_grad.reshape(tokens, model_width)
    query_weight_grad = across(first_low, query_grad_low)
    query_bias_grad = column_sum(query_grad_low)
    key_weight_grad = across(first_low, key_grad_low)
    value_weight_grad = across(first_low, value_grad_low)
    value_bias_grad = column_sum(value_grad_low)
    grad_first = (
        against(query_grad_low, query_weight)
        + against(key_grad_low, key_weight)
        + against(value_grad_low, value_weight)
    )
    first_back, first_gain_grad, first_shift_grad = norm_backward(
        grad_first, first_normed, first_inverse, first_gain.astype(floats)
    )
    atoms_grad = (
        (grad_middle + first_back).astype(halves).reshape(molecules, atom_rows, model_width)
    )
    (
        first_gain_grad,
        first_shift_grad,
        query_weight_grad,
        query_bias_grad,
        key_weight_grad,
        value_weight_grad,
        value_bias_grad,
        out_weight_grad,
        out_bias_grad,
        second_gain_grad,
        second_shift_grad,
        inner_weight_grad,
        inner_bias_grad,
        outer_weight_grad,
        outer_bias_grad,
    ) = (
        lax.psum_scatter(first_gain_grad, "batch", scatter_dimension=0, tiled=True),
        lax.psum_scatter(first_shift_grad, "batch", scatter_dimension=0, tiled=True),
        lax.psum_scatter(query_weight_grad, "batch", scatter_dimension=0, tiled=True),
        lax.psum_scatter(query_bias_grad, "batch", scatter_dimension=0, tiled=True),
        lax.psum_scatter(key_weight_grad, "batch", scatter_dimension=0, tiled=True),
        lax.psum_scatter(value_weight_grad, "batch", scatter_dimension=0, tiled=True),
        lax.psum_scatter(value_bias_grad, "batch", scatter_dimension=0, tiled=True),
        lax.psum_scatter(out_weight_grad, "batch", scatter_dimension=0, tiled=True),
        lax.psum_scatter(out_bias_grad, "batch", scatter_dimension=0, tiled=True),
        lax.psum_scatter(second_gain_grad, "batch", scatter_dimension=0, tiled=True),
        lax.psum_scatter(second_shift_grad, "batch", scatter_dimension=0, tiled=True),
        lax.psum_scatter(inner_weight_grad, "batch", scatter_dimension=0, tiled=True),
        lax.psum_scatter(inner_bias_grad, "batch", scatter_dimension=0, tiled=True),
        lax.psum_scatter(outer_weight_grad, "batch", scatter_dimension=0, tiled=True),
        lax.psum_scatter(outer_bias_grad, "batch", scatter_dimension=0, tiled=True),
    )
    (
        first_gain_grad,
        first_shift_grad,
        query_weight_grad,
        query_bias_grad,
        key_weight_grad,
        value_weight_grad,
        value_bias_grad,
        out_weight_grad,
        out_bias_grad,
        second_gain_grad,
        second_shift_grad,
        inner_weight_grad,
        inner_bias_grad,
        outer_weight_grad,
        outer_bias_grad,
    ) = (
        lax.psum(first_gain_grad.astype(jnp.bfloat16), "rows").astype(jnp.float32),
        lax.psum(first_shift_grad.astype(jnp.bfloat16), "rows").astype(jnp.float32),
        lax.psum(query_weight_grad.astype(jnp.bfloat16), "rows").astype(jnp.float32),
        lax.psum(query_bias_grad.astype(jnp.bfloat16), "rows").astype(jnp.float32),
        lax.psum(key_weight_grad.astype(jnp.bfloat16), "rows").astype(jnp.float32),
        lax.psum(value_weight_grad.astype(jnp.bfloat16), "rows").astype(jnp.float32),
        lax.psum(value_bias_grad.astype(jnp.bfloat16), "rows").astype(jnp.float32),
        lax.psum(out_weight_grad.astype(jnp.bfloat16), "rows").astype(jnp.float32),
        lax.psum(out_bias_grad.astype(jnp.bfloat16), "rows").astype(jnp.float32),
        lax.psum(second_gain_grad.astype(jnp.bfloat16), "rows").astype(jnp.float32),
        lax.psum(second_shift_grad.astype(jnp.bfloat16), "rows").astype(jnp.float32),
        lax.psum(inner_weight_grad.astype(jnp.bfloat16), "rows").astype(jnp.float32),
        lax.psum(inner_bias_grad.astype(jnp.bfloat16), "rows").astype(jnp.float32),
        lax.psum(outer_weight_grad.astype(jnp.bfloat16), "rows").astype(jnp.float32),
        lax.psum(outer_bias_grad.astype(jnp.bfloat16), "rows").astype(jnp.float32),
    )
    return (
        atoms_out,
        pair_out,
        atoms_grad,
        pair_grad,
        first_gain_grad,
        first_shift_grad,
        query_weight_grad,
        query_bias_grad,
        key_weight_grad,
        value_weight_grad,
        value_bias_grad,
        out_weight_grad,
        out_bias_grad,
        second_gain_grad,
        second_shift_grad,
        inner_weight_grad,
        inner_bias_grad,
        outer_weight_grad,
        outer_bias_grad,
    )


def solution(mesh):
    placed = (
        P("batch", "rows", None),
        P("batch", None, "rows", None),
        P("batch"),
        P(),
        P(),
        P(),
        P(),
        P(),
        P(),
        P(),
        P(),
        P(),
        P(),
        P(),
        P(),
        P(),
        P(),
        P(),
        P("batch", "rows", None),
        P("batch", None, "rows", None),
    )
    return jax.shard_map(
        shards,
        mesh=mesh,
        in_specs=placed,
        out_specs=(
            P("batch", "rows", None),
            P("batch", None, "rows", None),
            P("batch", "rows", None),
            P("batch", None, "rows", None),
            P("batch"),
            P("batch"),
            P("batch", None),
            P("batch"),
            P("batch", None),
            P("batch", None),
            P("batch"),
            P("batch", None),
            P("batch"),
            P("batch"),
            P("batch"),
            P("batch", None),
            P("batch"),
            P("batch", None),
            P("batch"),
        ),
        check_vma=False,
    )
```

profile of v0, /device:TPU:0, one launch (start us, length us, event | category | flops | bytes accessed | tf_op | source)
XLA Modules:
  0.0 693.5 jit_solution(6744688574644620447)
XLA Ops:
  25.2 20.6 %all-gather.5.cloned.1.call-done = bf16[4,256,512]{2,1,0:T(8,128)(2,1)} async-done(((bf16[4,64,512]{2,1,0:T(8,128)(2,1)}), bf16[4,256,512]{2,1,0:T(8,128)(2,1)}) %all-gather.5.cloned.1.call-update) | async-done | bytes 1048592 | tf_op jit(solution)/shard_map/all_gather | solution.py:147
  48.2 27.3 %all-gather.3.cloned.1.call-done = bf16[4,256,512]{2,1,0:T(8,128)(2,1)} async-done(((bf16[4,64,512]{2,1,0:T(8,128)(2,1)}), bf16[4,256,512]{2,1,0:T(8,128)(2,1)}) %all-gather.3.cloned.1.call-update) | async-done | bytes 1048592 | tf_op jit(solution)/shard_map/all_gather | solution.py:146
  77.8 4.5 broadcast.188.clone
  82.3 43.1 %while.30 = (s32[]{:T(128)}, bf16[4,64,64,256]{3,2,1,0:T(8,128)(2,1)}, bf16[4,64,64,8]{1,3,2,0:T(8,128)(2,1)}, f32[4,64,64]{2,1,0:T(8,128)S(1)}, bf16[4,64,64,8]...) while((s32[]{:T(128)}, ...), condition=%wide.region_5.6_spmd, body=%wide.region_2.5_spmd.sunk | while | flops 47214848 | bytes 21941888 | solution.py:153
  132.1 4.8 convert_reduce_fusion
  145.5 124.5 %while.31 = (s32[]{:T(128)}, bf16[4,64,64,256]{3,2,1,0:T(8,128)(2,1)}, bf16[4,64,64,8]{1,3,2,0:T(8,128)(2,1)}, f32[4,256,64,8]{1,3,2,0:T(8,128)}, f32[4,256,64,8...) while((s32[]{:T(128)}, ...), condition=%wide.region_12.13_spmd, body=%wide.region_10.12_spmd.sunk | while | flops 193147904 | bytes 48575392 | solution.py:193
  147.4 5.2 fusion.229
  152.5 6.8 fusion.230
  162.7 7.0 %fusion.231 = f32[4,256,64,8]{1,3,2,0:T(8,128)} fusion(f32[4,256,64,8]{1,3,2,0:T(8,128)} %get-tuple-element.487, s32[]{:T(128)S(6)} %copy.94, f32[64,64,256]{2,1,0:T(8,128)} %fusion.229, bf16[4,64,64,256]{3,2,1,0:T(8,128)(2,1)} %get-tuple-element.510, bf16[4,256,64,8]{1,3,2,0:T(8,128)(2,1)S(1)} %get-tuple-element.509, ...), kind=kOutput, calls=%fused_computation.37.clone.1 | convolution fusion | flops 56758528 | bytes 11931136 | tf_op jit(solution)/shard_map/while/body/eval_jaxpr/hij,ihe->jhe/dot_general | solution.py:100
  169.6 6.9 %bitcast_dynamic-update-slice_fusion.8 = bf16[4,64,64,256]{3,2,1,0:T(8,128)(2,1)} fusion(bf16[4,64,64,256]{3,2,1,0:T(8,128)(2,1)} %get-tuple-element.485, s32[]{:T(128)S(6)} %copy.94, bf16[4,64,64,256]{3,2,1,0:T(8,128)(2,1)} %get-tuple-element.510, f32[64,64,256]{2,1,0:T(8,128)} %fusion.229, bf16[4,256,64,8]{1,3,2,0:T(8,128)(2,1)S(1)} %get-tuple-element.509, ...), kind=kOutput, calls=%fused_computation.30.clone.1 | convolution fusion | flops 39850240 | bytes 13371904 | tf_op jit(solution)/shard_map/while/body/eval_jaxpr/sub | solution.py:94
  178.5 5.1 fusion.229
  183.6 6.8 fusion.230
  193.8 7.0 %fusion.231 = f32[4,256,64,8]{1,3,2,0:T(8,128)} fusion(f32[4,256,64,8]{1,3,2,0:T(8,128)} %get-tuple-element.487, s32[]{:T(128)S(6)} %copy.94, f32[64,64,256]{2,1,0:T(8,128)} %fusion.229, bf16[4,64,64,256]{3,2,1,0:T(8,128)(2,1)} %get-tuple-element.510, bf16[4,256,64,8]{1,3,2,0:T(8,128)(2,1)S(1)} %get-tuple-element.509, ...), kind=kOutput, calls=%fused_computation.37.clone.1 | convolution fusion | flops 56758528 | bytes 11931136 | tf_op jit(solution)/shard_map/while/body/eval_jaxpr/hij,ihe->jhe/dot_general | solution.py:100
  200.8 6.9 %bitcast_dynamic-update-slice_fusion.8 = bf16[4,64,64,256]{3,2,1,0:T(8,128)(2,1)} fusion(bf16[4,64,64,256]{3,2,1,0:T(8,128)(2,1)} %get-tuple-element.485, s32[]{:T(128)S(6)} %copy.94, bf16[4,64,64,256]{3,2,1,0:T(8,128)(2,1)} %get-tuple-element.510, f32[64,64,256]{2,1,0:T(8,128)} %fusion.229, bf16[4,256,64,8]{1,3,2,0:T(8,128)(2,1)S(1)} %get-tuple-element.509, ...), kind=kOutput, calls=%fused_computation.30.clone.1 | convolution fusion | flops 39850240 | bytes 13371904 | tf_op jit(solution)/shard_map/while/body/eval_jaxpr/sub | solution.py:94
  209.6 5.2 fusion.229
  214.8 6.8 fusion.230
  224.9 7.0 %fusion.231 = f32[4,256,64,8]{1,3,2,0:T(8,128)} fusion(f32[4,256,64,8]{1,3,2,0:T(8,128)} %get-tuple-element.487, s32[]{:T(128)S(6)} %copy.94, f32[64,64,256]{2,1,0:T(8,128)} %fusion.229, bf16[4,64,64,256]{3,2,1,0:T(8,128)(2,1)} %get-tuple-element.510, bf16[4,256,64,8]{1,3,2,0:T(8,128)(2,1)S(1)} %get-tuple-element.509, ...), kind=kOutput, calls=%fused_computation.37.clone.1 | convolution fusion | flops 56758528 | bytes 11931136 | tf_op jit(solution)/shard_map/while/body/eval_jaxpr/hij,ihe->jhe/dot_general | solution.py:100
  231.9 6.9 %bitcast_dynamic-update-slice_fusion.8 = bf16[4,64,64,256]{3,2,1,0:T(8,128)(2,1)} fusion(bf16[4,64,64,256]{3,2,1,0:T(8,128)(2,1)} %get-tuple-element.485, s32[]{:T(128)S(6)} %copy.94, bf16[4,64,64,256]{3,2,1,0:T(8,128)(2,1)} %get-tuple-element.510, f32[64,64,256]{2,1,0:T(8,128)} %fusion.229, bf16[4,256,64,8]{1,3,2,0:T(8,128)(2,1)S(1)} %get-tuple-element.509, ...), kind=kOutput, calls=%fused_computation.30.clone.1 | convolution fusion | flops 39850240 | bytes 13371904 | tf_op jit(solution)/shard_map/while/body/eval_jaxpr/sub | solution.py:94
  240.7 5.2 fusion.229
  245.9 6.8 fusion.230
  256.1 7.0 %fusion.231 = f32[4,256,64,8]{1,3,2,0:T(8,128)} fusion(f32[4,256,64,8]{1,3,2,0:T(8,128)} %get-tuple-element.487, s32[]{:T(128)S(6)} %copy.94, f32[64,64,256]{2,1,0:T(8,128)} %fusion.229, bf16[4,64,64,256]{3,2,1,0:T(8,128)(2,1)} %get-tuple-element.510, bf16[4,256,64,8]{1,3,2,0:T(8,128)(2,1)S(1)} %get-tuple-element.509, ...), kind=kOutput, calls=%fused_computation.37.clone.1 | convolution fusion | flops 56758528 | bytes 11931136 | tf_op jit(solution)/shard_map/while/body/eval_jaxpr/hij,ihe->jhe/dot_general | solution.py:100
  263.0 6.9 %bitcast_dynamic-update-slice_fusion.8 = bf16[4,64,64,256]{3,2,1,0:T(8,128)(2,1)} fusion(bf16[4,64,64,256]{3,2,1,0:T(8,128)(2,1)} %get-tuple-element.485, s32[]{:T(128)S(6)} %copy.94, bf16[4,64,64,256]{3,2,1,0:T(8,128)(2,1)} %get-tuple-element.510, f32[64,64,256]{2,1,0:T(8,128)} %fusion.229, bf16[4,256,64,8]{1,3,2,0:T(8,128)(2,1)S(1)} %get-tuple-element.509, ...), kind=kOutput, calls=%fused_computation.30.clone.1 | convolution fusion | flops 39850240 | bytes 13371904 | tf_op jit(solution)/shard_map/while/body/eval_jaxpr/sub | solution.py:94
  280.7 35.7 %reduce-scatter.11.cloned.1.call-done = f32[4,64,512]{2,1,0:T(8,128)} async-done(((f32[4,256,512]{2,1,0:T(8,128)}), f32[4,64,512]{2,1,0:T(8,128)}) %reduce-scatter.11.cloned.1.call-update) | async-done | bytes 524304 | tf_op jit(solution)/shard_map/reduce_scatter | solution.py:213
  319.0 43.0 %reduce-scatter.9.cloned.1.call-done = f32[4,64,512]{2,1,0:T(8,128)} async-done(((f32[4,256,512]{2,1,0:T(8,128)}), f32[4,64,512]{2,1,0:T(8,128)}) %reduce-scatter.9.cloned.1.call-update) | async-done | bytes 524304 | tf_op jit(solution)/shard_map/reduce_scatter | solution.py:207
  379.3 20.9 %reduce-scatter.19.cloned.1.call-done = f32[64,512]{1,0:T(8,128)} async-done(((f32[512,512]{1,0:T(8,128)}), f32[64,512]{1,0:T(8,128)}) %reduce-scatter.19.cloned.1.call-update) | async-done | bytes 131088 | tf_op jit(solution)/shard_map/reduce_scatter | solution.py:263
  401.8 37.5 %reduce-scatter.13.cloned.1.call-done = f32[64,512]{1,0:T(8,128)} async-done(((f32[512,512]{1,0:T(8,128)}), f32[64,512]{1,0:T(8,128)}) %reduce-scatter.13.cloned.1.call-update) | async-done | bytes 131088 | tf_op jit(solution)/shard_map/reduce_scatter | solution.py:258
  442.1 36.5 %reduce-scatter.17.cloned.1.call-done = f32[64,512]{1,0:T(8,128)} async-done(((f32[512,512]{1,0:T(8,128)}), f32[64,512]{1,0:T(8,128)}) %reduce-scatter.17.cloned.1.call-update) | async-done | bytes 131088 | tf_op jit(solution)/shard_map/reduce_scatter | solution.py:261
  480.1 37.7 %reduce-scatter.15.cloned.1.call-done = f32[64,512]{1,0:T(8,128)} async-done(((f32[512,512]{1,0:T(8,128)}), f32[64,512]{1,0:T(8,128)}) %reduce-scatter.15.cloned.1.call-update) | async-done | bytes 131088 | tf_op jit(solution)/shard_map/reduce_scatter | solution.py:260
  519.3 53.2 %reduce-scatter.23.cloned.1.call-done = f32[256,512]{1,0:T(8,128)} async-done(((f32[2048,512]{1,0:T(8,128)}), f32[256,512]{1,0:T(8,128)}) %reduce-scatter.23.cloned.1.call-update) | async-done | bytes 524304 | tf_op jit(solution)/shard_map/reduce_scatter | solution.py:269
  574.3 53.1 %reduce-scatter.21.cloned.1.call-done = f32[64,2048]{1,0:T(8,128)} async-done(((f32[512,2048]{1,0:T(8,128)}), f32[64,2048]{1,0:T(8,128)}) %reduce-scatter.21.cloned.1.call-update) | async-done | bytes 524304 | tf_op jit(solution)/shard_map/reduce_scatter | solution.py:267
  631.8 24.1 %all-reduce.9 = (bf16[512]{0:T(512)(128)(2,1)S(1)}, bf16[512]{0:T(512)(128)(2,1)S(1)}, bf16[512]{0:T(512)(128)(2,1)S(1)}, bf16[512]{0:T(512)(128)(2,1)S(1)}, bf1...) all-reduce(f32[512]{0:T(512)S(1)} %get-tuple-element.213, ...), channel_id=4, replica_groups=mesh['batch'=8,'rows'=4] {'batch'}, use_global_device_ids=true, to_apply=%region_18.19.clone | all-reduce | flops 6144 | bytes 36864
  656.6 12.1 %all-reduce.10 = (bf16[64]{0:T(256)(128)(2,1)S(1)}, bf16[64]{0:T(256)(128)(2,1)S(1)}, bf16[64]{0:T(256)(128)(2,1)S(1)}, bf16[64]{0:T(256)(128)(2,1)S(1)}, bf16[6...) all-reduce(bf16[64]{0:T(256)(128)(2,1)S(1)} %dynamic-slice.35, ...), channel_id=1, replica_groups=mesh['batch'=8,'rows'=4] {'rows'}, use_global_device_ids=true, to_apply=%region_19.20 | all-reduce | flops 768 | bytes 3072 | tf_op jit(solution)/shard_map/psum | solution.py:289
  (257 shorter events, 163.2 us)
Async XLA Ops:
  7.2 124.8 %copy-start = (bf16[512,2048]{1,0:T(8,128)(2,1)S(1)}, bf16[512,2048]{1,0:T(8,128)(2,1)}, u32[]{:S(2)}) copy-start(bf16[512,2048]{1,0:T(8,128)(2,1)} %param.38) | copy-start | bytes 6291460
  7.2 9.9 %copy-start.5 = (bf16[4,64,512]{2,1,0:T(8,128)(2,1)S(1)}, bf16[4,64,512]{2,1,0:T(8,128)(2,1)}, u32[]{:S(2)}) copy-start(bf16[4,64,512]{2,1,0:T(8,128)(2,1)} %param.24) | copy-start | bytes 786436
  7.2 9.2 %copy-start.41 = (bf16[512]{0:T(512)(128)(2,1)S(1)}, bf16[512]{0:T(512)(128)(2,1)}, u32[]{:S(2)}) copy-start(bf16[512]{0:T(512)(128)(2,1)} %param.37) | copy-start | bytes 3076
  7.3 9.2 %copy-start.42 = (bf16[512]{0:T(512)(128)(2,1)S(1)}, bf16[512]{0:T(512)(128)(2,1)}, u32[]{:S(2)}) copy-start(bf16[512]{0:T(512)(128)(2,1)} %param.30) | copy-start | bytes 3076
  7.3 9.2 %copy-start.43 = (bf16[512]{0:T(512)(128)(2,1)S(1)}, bf16[512]{0:T(512)(128)(2,1)}, u32[]{:S(2)}) copy-start(bf16[512]{0:T(512)(128)(2,1)} %param.35) | copy-start | bytes 3076
  7.3 9.2 %copy-start.37 = (bf16[2048]{0:T(1024)(128)(2,1)S(1)}, bf16[2048]{0:T(1024)(128)(2,1)}, u32[]{:S(2)}) copy-start(bf16[2048]{0:T(1024)(128)(2,1)} %param.39) | copy-start | bytes 12292
  7.3 38.6 %all-gather.5.cloned.1.call-start = ((), (), s32[]{:S(2)}) async-start(), calls=%async_computation.9 | async-start | bytes 1310720 | tf_op jit(solution)/shard_map/all_gather | solution.py:147
  15.1 60.4 %all-gather.3.cloned.1.call-start = ((), (), s32[]{:S(2)}) async-start(), calls=%async_computation.8 | async-start | bytes 1310720 | tf_op jit(solution)/shard_map/all_gather | solution.py:146
  16.2 300.3 %reduce-scatter.11.cloned.1.call-start = ((), (), s32[]{:S(2)}) async-start(), calls=%async_computation.11 | async-start | bytes 2621440 | tf_op jit(solution)/shard_map/reduce_scatter | solution.py:213
  139.1 136.9 %copy-start.8 = (f32[256,512]{1,0:T(8,128)}, f32[256,512]{1,0:T(8,128)S(1)}, u32[]{:S(2)}) copy-start(f32[256,512]{1,0:T(8,128)S(1)} %get-tuple-element.290) | copy-start | bytes 1572868
  272.9 89.0 %reduce-scatter.9.cloned.1.call-start = ((), (), s32[]{:S(2)}) async-start(), calls=%async_computation.10 | async-start | bytes 2621440 | tf_op jit(solution)/shard_map/reduce_scatter | solution.py:207
  275.9 124.3 %reduce-scatter.19.cloned.1.call-start = ((), (), s32[]{:S(2)}) async-start(), calls=%async_computation.15 | async-start | bytes 1179648 | tf_op jit(solution)/shard_map/reduce_scatter | solution.py:263
  278.2 161.2 %reduce-scatter.13.cloned.1.call-start = ((), (), s32[]{:S(2)}) async-start(), calls=%async_computation.12 | async-start | bytes 1179648 | tf_op jit(solution)/shard_map/reduce_scatter | solution.py:258
  279.2 39.6 %copy-start.16 = (bf16[256,512]{0,1:T(8,128)(2,1)}, bf16[256,512]{0,1:T(8,128)(2,1)S(1)}, u32[]{:S(2)}) copy-start(bf16[256,512]{0,1:T(8,128)(2,1)S(1)} %reshape.266) | copy-start | bytes 786436
  280.7 197.9 %reduce-scatter.17.cloned.1.call-start = ((), (), s32[]{:S(2)}) async-start(), calls=%async_computation.14 | async-start | bytes 1179648 | tf_op jit(solution)/shard_map/reduce_scatter | solution.py:261
  318.9 46.2 %copy-start.10 = (f32[256,2048]{1,0:T(8,128)S(1)}, f32[256,2048]{1,0:T(8,128)}, u32[]{:S(2)}) copy-start(f32[256,2048]{1,0:T(8,128)} %get-tuple-element.297) | copy-start | bytes 6291460
  318.9 46.2 %copy-start.14 = (bf16[4,64,512]{2,1,0:T(8,128)(2,1)S(1)}, bf16[4,64,512]{2,1,0:T(8,128)(2,1)}, u32[]{:S(2)}) copy-start(bf16[4,64,512]{2,1,0:T(8,128)(2,1)} %param.42) | copy-start | bytes 786436
  318.9 198.9 %reduce-scatter.15.cloned.1.call-start = ((), (), s32[]{:S(2)}) async-start(), calls=%async_computation.13 | async-start | bytes 1179648 | tf_op jit(solution)/shard_map/reduce_scatter | solution.py:260
  365.0 207.5 %reduce-scatter.23.cloned.1.call-start = ((), (), s32[]{:S(2)}) async-start(), calls=%async_computation.17 | async-start | bytes 4718592 | tf_op jit(solution)/shard_map/reduce_scatter | solution.py:269
  368.0 259.4 %reduce-scatter.21.cloned.1.call-start = ((), (), s32[]{:S(2)}) async-start(), calls=%async_computation.16 | async-start | bytes 4718592 | tf_op jit(solution)/shard_map/reduce_scatter | solution.py:267
  372.2 305.2 %all-reduce.14.cloned.1.call-start = ((), (), s32[]{:S(2)}) async-start(), calls=%async_computation.18 | async-start | bytes 1572864 | tf_op jit(solution)/shard_map/psum | solution.py:291
  375.5 65.5 %copy-start.19 = (bf16[4,64,512]{2,1,0:T(8,128)(2,1)S(1)}, bf16[4,64,512]{2,1,0:T(8,128)(2,1)}, u32[]{:S(2)}) copy-start(bf16[4,64,512]{2,1,0:T(8,128)(2,1)} %copy-done.18) | copy-start | bytes 786436
  375.5 65.4 %copy-start.21 = (bf16[512,512]{1,0:T(8,128)(2,1)S(1)}, bf16[512,512]{1,0:T(8,128)(2,1)}, u32[]{:S(2)}) copy-start(bf16[512,512]{1,0:T(8,128)(2,1)} %param.31) | copy-start | bytes 1572868
  440.9 188.3 %copy-start.28 = (bf16[4,64,512]{2,1,0:T(8,128)(2,1)S(1)}, bf16[4,64,512]{2,1,0:T(8,128)(2,1)}, u32[]{:S(2)}) copy-start(bf16[4,64,512]{2,1,0:T(8,128)(2,1)} %copy-done.27) | copy-start | bytes 786436
  440.9 188.3 %copy-start.32 = (f32[256]{0:T(256)S(1)}, f32[256]{0:T(256)}, u32[]{:S(2)}) copy-start(f32[256]{0:T(256)} %copy-done.31) | copy-start | bytes 3076
  440.9 188.3 %copy-start.34 = (f32[256]{0:T(256)S(1)}, f32[256]{0:T(256)}, u32[]{:S(2)}) copy-start(f32[256]{0:T(256)} %copy-done.33) | copy-start | bytes 3076
  574.3 57.5 %copy-start.35 = (f32[512]{0:T(512)S(1)}, f32[512]{0:T(512)}, u32[]{:S(2)}) copy-start(f32[512]{0:T(512)} %get-tuple-element.289) | copy-start | bytes 6148
  574.3 57.5 %copy-start.36 = (f32[2048]{0:T(1024)S(1)}, f32[2048]{0:T(1024)}, u32[]{:S(2)}) copy-start(f32[2048]{0:T(1024)} %get-tuple-element.287) | copy-start | bytes 24580
  574.3 57.5 %copy-start.38 = (f32[512]{0:T(512)S(1)}, f32[512]{0:T(512)}, u32[]{:S(2)}) copy-start(f32[512]{0:T(512)} %get-tuple-element.211) | copy-start | bytes 6148
  574.3 57.5 %copy-start.39 = (f32[512]{0:T(512)S(1)}, f32[512]{0:T(512)}, u32[]{:S(2)}) copy-start(f32[512]{0:T(512)} %get-tuple-element.217) | copy-start | bytes 6148
  574.3 99.1 %copy-start.9 = (f32[256,512]{1,0:T(8,128)S(1)}, f32[256,512]{1,0:T(8,128)}, u32[]{:S(2)}) copy-start(f32[256,512]{1,0:T(8,128)} %copy-done.8) | copy-start | bytes 1572868
  629.2 57.8 %copy-start.1 = (bf16[512,2048]{1,0:T(8,128)(2,1)S(1)}, bf16[512,2048]{1,0:T(8,128)(2,1)}, u32[]{:S(2)}) copy-start(bf16[512,2048]{1,0:T(8,128)(2,1)} %param.38) | copy-start | bytes 6291460
  (25 other events, 74.1 us)
Sparse Core Ops, SparseCore 0:
  15.2 30.6 all-gather.4
  48.0 27.4 all-gather.2
  273.1 43.3 reduce-scatter.10
  318.7 43.1 reduce-scatter.8
  364.9 35.3 reduce-scatter.18
  403.3 35.9 reduce-scatter.12
  442.5 35.9 reduce-scatter.16
  481.7 35.9 reduce-scatter.14
  521.1 51.3 reduce-scatter.22
  576.1 51.2 reduce-scatter.20
  631.4 45.9 all-reduce.13
where the time goes:
time: 696 us; the launch traced here: 694 us
  waiting for transfers between devices  368 us (53%)
  matrix products  179 us (26%)
  other arithmetic  49.1 us (7%)
  local copies, waits for them, and re-layouts  44.4 us (6%)
  blocking collectives  36.2 us (5%)
  between operations  15.8 us (2%)
    reduce_scatter x1, waiting for transfers between devices, shards(): lax.psum_scatter(outer_weight_grad, 'batch', scatter_dimension=0, tiled=T...  53.2 us
    reduce_scatter x1, waiting for transfers between devices, shards(): lax.psum_scatter(inner_weight_grad, 'batch', scatter_dimension=0, tiled=T...  53.1 us
    reduce_scatter x1, waiting for transfers between devices, shards(): lax.psum_scatter(key_grad.reshape(molecules, key_count, model_width), 'ro...  43 us
    reduce_scatter x1, waiting for transfers between devices, shards(): lax.psum_scatter(key_weight_grad, 'batch', scatter_dimension=0, tiled=True)  37.7 us
    reduce_scatter x1, waiting for transfers between devices, shards(): lax.psum_scatter(query_weight_grad, 'batch', scatter_dimension=0, tiled=T...  37.5 us
    reduce_scatter x1, waiting for transfers between devices, shards(): lax.psum_scatter(value_weight_grad, 'batch', scatter_dimension=0, tiled=T...  36.5 us
    dot_general x8, matrix products, scores_of(): jnp.einsum('ihe,jhe->hij', query_rows, key_rows, preferred_element_type=j...  35.8 us
    reduce_scatter x1, waiting for transfers between devices, shards(): lax.psum_scatter(value_grad.reshape(molecules, key_count, model_width), '...  35.7 us
  transfers between devices with their start and end apart: 11, of which 11 were waited for; matrix products, arithmetic and copies ran while one was open for 8% of the time, Pallas kernels for 0%

commit v1 on v0

--- a/solution.py
+++ b/solution.py
@@ -6,6 +6,26 @@
 
 EPSILON = 1e-05
 MASKED = -1000000000.0
+
+
+def render_the_ways(patch):
+    axis_total = jax.lax.axis_size("rows")
+    built = range(axis_total)
+    z_new = map(lambda u: (u, (u + 1) % axis_total), built)
+    line_up = list(z_new)
+    part_next = range(axis_total)
+    res = map(lambda u: (u, (u - 1) % axis_total), part_next)
+    all_rows = list(res)
+    formed, arr_out = ([patch], [patch])
+    for _ in range(axis_total // 2):
+        v_now = jax.lax.ppermute(formed[-1], "rows", line_up)
+        formed.append(v_now)
+    for _ in [*range((axis_total - 1) // 2)]:
+        w1 = jax.lax.ppermute(arr_out[-1], "rows", all_rows)
+        arr_out.append(w1)
+    t1 = jnp.concatenate([*formed[::-1], *arr_out[1:]], 1)
+    vec_out = jax.lax.axis_index("rows")
+    return jnp.roll(t1, (vec_out - axis_total // 2) * patch.shape[1], 1)
 
 
 def norm_forward(values_in, gain, shift):
@@ -144,7 +164,7 @@
     key_local, value_local = project_keys(first_grouped, key_weight, value_weight, value_bias)
     all_keys, all_values = (
         lax.all_gather(key_local, "rows", axis=1, tiled=True),
-        lax.all_gather(value_local, "rows", axis=1, tiled=True),
+        render_the_ways(value_local),
     )
     key_count = all_keys.shape[1]
     query_heads = query_low.reshape(molecules, atom_rows, head_count, head_size)

time: 696 us -> 678 us (0.974)
  waiting for transfers between devices: 368 us -> 337 us
  starting transfers between devices: 0.68 us -> 8.29 us
    all_gather x1, waiting for transfers between devices: 27.3 us -> 2.6 us  [shards(): lax.all_gather(key_local, 'rows', axis=1, tiled=True)]
    all_gather x1 -> x0, waiting for transfers between devices: 20.6 us -> none  [shards(): lax.all_gather(value_local, 'rows', axis=1, tiled=True)]
    ppermute x0 -> x3, waiting for transfers between devices: none -> 13.2 us  [the longest x2 13.2 us: render_the_ways(): v_now = jax.lax.ppermute(formed[-1], 'rows', line_up)]
    ppermute x0 -> x3, starting transfers between devices: none -> 7.66 us  [the longest x1 5.1 us: render_the_ways(): w1 = jax.lax.ppermute(arr_out[-1], 'rows', all_rows)]
  transfers between devices with their start and end apart: 11 -> 13, of which waited for: 11 -> 12; matrix products, arithmetic and copies ran while one was open for 8% -> 9% of each run, Pallas kernels for 0% -> 0%
where the time goes in v1:
time: 678 us; the launch traced here: 676 us
  waiting for transfers between devices  337 us (50%)
  matrix products  179 us (26%)
  other arithmetic  51.2 us (8%)
  local copies, waits for them, and re-layouts  47.8 us (7%)
  blocking collectives  36.2 us (5%)
  between operations  16.1 us (2%)
  starting transfers between devices  8.29 us (1%)
    reduce_scatter x1, waiting for transfers between devices, shards(): lax.psum_scatter(inner_weight_grad, 'batch', scatter_dimension=0, tiled=T...  53.3 us
    reduce_scatter x1, waiting for transfers between devices, shards(): lax.psum_scatter(outer_weight_grad, 'batch', scatter_dimension=0, tiled=T...  53.1 us
    reduce_scatter x1, waiting for transfers between devices, shards(): lax.psum_scatter(key_grad.reshape(molecules, key_count, model_width), 'ro...  43.2 us
    reduce_scatter x1, waiting for transfers between devices, shards(): lax.psum_scatter(key_weight_grad, 'batch', scatter_dimension=0, tiled=True)  37.7 us
    reduce_scatter x1, waiting for transfers between devices, shards(): lax.psum_scatter(query_weight_grad, 'batch', scatter_dimension=0, tiled=T...  37.5 us
    reduce_scatter x1, waiting for transfers between devices, shards(): lax.psum_scatter(value_grad.reshape(molecules, key_count, model_width), '...  37.3 us
    reduce_scatter x1, waiting for transfers between devices, shards(): lax.psum_scatter(value_weight_grad, 'batch', scatter_dimension=0, tiled=T...  36.4 us
    dot_general x8, matrix products, scores_of(): jnp.einsum('ihe,jhe->hij', query_rows, key_rows, preferred_element_type=j...  35.8 us
  transfers between devices with their start and end apart: 13, of which 12 were waited for; matrix products, arithmetic and copies ran while one was open for 9% of the time, Pallas kernels for 0%

profile of v1, /device:TPU:0, one launch (start us, length us, event | category | flops | bytes accessed | tf_op | source)
XLA Modules:
  0.0 675.8 jit_solution(6675213570879709359)
XLA Ops:
  14.4 5.1 collective-permute-start.2
  37.9 9.8 %collective-permute-done.1 = bf16[4,64,512]{2,1,0:T(8,128)(2,1)S(1)} collective-permute-done((bf16[4,64,512]{2,1,0:T(8,128)(2,1)}, bf16[4,64,512]{2,1,0:T(8,128)(2,1)S(1)}, u32[]{:S(2)}, u32[]{:S(2)}) %collective-permute-start.1) | collective-permute-done | bytes 262176 | tf_op jit(solution)/shard_map/ppermute | solution.py:21
  58.0 4.5 broadcast.189.clone
  62.5 43.1 %while.30 = (s32[]{:T(128)}, bf16[4,64,64,256]{3,2,1,0:T(8,128)(2,1)}, bf16[4,64,64,8]{1,3,2,0:T(8,128)(2,1)}, f32[4,64,64]{2,1,0:T(8,128)S(1)}, bf16[4,64,64,8]...) while((s32[]{:T(128)}, ...), condition=%wide.region_5.6_spmd, body=%wide.region_2.5_spmd.sunk | while | flops 47214848 | bytes 21941888 | solution.py:173
  112.3 4.8 convert_reduce_fusion
  125.7 124.5 %while.31 = (s32[]{:T(128)}, bf16[4,64,64,256]{3,2,1,0:T(8,128)(2,1)}, bf16[4,64,64,8]{1,3,2,0:T(8,128)(2,1)}, f32[4,256,64,8]{1,3,2,0:T(8,128)}, f32[4,256,64,8...) while((s32[]{:T(128)}, ...), condition=%wide.region_12.13_spmd, body=%wide.region_10.12_spmd.sunk | while | flops 193147904 | bytes 48575392 | solution.py:213
  127.6 5.1 fusion.229
  132.8 6.8 %fusion.230 = bf16[4,64,64,8]{1,3,2,0:T(8,128)(2,1)} fusion(bf16[4,64,64,8]{1,3,2,0:T(8,128)(2,1)} %get-tuple-element.486, s32[]{:T(128)S(6)} %copy.99, bf16[4,256,64,8]{1,3,2,0:T(8,128)(2,1)S(1)} %get-tuple-element.505, f32[64,64,256]{2,1,0:T(8,128)} %fusion.229, bf16[4,64,64,256]{3,2,1,0:T(8,128)(2,1)} %get-tuple-element.510, ...), kind=kOutput, calls=%fused_computation.41.clone.1 | convolution fusion | flops 56692992 | bytes 11668992 | tf_op jit(solution)/shard_map/while/body/eval_jaxpr/hij,jhe->ihe/dot_general | solution.py:117
  142.9 7.0 %fusion.231 = f32[4,256,64,8]{1,3,2,0:T(8,128)} fusion(f32[4,256,64,8]{1,3,2,0:T(8,128)} %get-tuple-element.487, s32[]{:T(128)S(6)} %copy.99, f32[64,64,256]{2,1,0:T(8,128)} %fusion.229, bf16[4,64,64,256]{3,2,1,0:T(8,128)(2,1)} %get-tuple-element.510, bf16[4,256,64,8]{1,3,2,0:T(8,128)(2,1)S(1)} %get-tuple-element.509, ...), kind=kOutput, calls=%fused_computation.37.clone.1 | convolution fusion | flops 56758528 | bytes 11931136 | tf_op jit(solution)/shard_map/while/body/eval_jaxpr/hij,ihe->jhe/dot_general | solution.py:120
  149.9 6.9 %bitcast_dynamic-update-slice_fusion.8 = bf16[4,64,64,256]{3,2,1,0:T(8,128)(2,1)} fusion(bf16[4,64,64,256]{3,2,1,0:T(8,128)(2,1)} %get-tuple-element.485, s32[]{:T(128)S(6)} %copy.99, bf16[4,64,64,256]{3,2,1,0:T(8,128)(2,1)} %get-tuple-element.510, f32[64,64,256]{2,1,0:T(8,128)} %fusion.229, bf16[4,256,64,8]{1,3,2,0:T(8,128)(2,1)S(1)} %get-tuple-element.509, ...), kind=kOutput, calls=%fused_computation.30.clone.1 | convolution fusion | flops 39850240 | bytes 13371904 | tf_op jit(solution)/shard_map/while/body/eval_jaxpr/sub | solution.py:114
  158.7 5.1 fusion.229
  163.9 6.8 %fusion.230 = bf16[4,64,64,8]{1,3,2,0:T(8,128)(2,1)} fusion(bf16[4,64,64,8]{1,3,2,0:T(8,128)(2,1)} %get-tuple-element.486, s32[]{:T(128)S(6)} %copy.99, bf16[4,256,64,8]{1,3,2,0:T(8,128)(2,1)S(1)} %get-tuple-element.505, f32[64,64,256]{2,1,0:T(8,128)} %fusion.229, bf16[4,64,64,256]{3,2,1,0:T(8,128)(2,1)} %get-tuple-element.510, ...), kind=kOutput, calls=%fused_computation.41.clone.1 | convolution fusion | flops 56692992 | bytes 11668992 | tf_op jit(solution)/shard_map/while/body/eval_jaxpr/hij,jhe->ihe/dot_general | solution.py:117
  174.1 7.0 %fusion.231 = f32[4,256,64,8]{1,3,2,0:T(8,128)} fusion(f32[4,256,64,8]{1,3,2,0:T(8,128)} %get-tuple-element.487, s32[]{:T(128)S(6)} %copy.99, f32[64,64,256]{2,1,0:T(8,128)} %fusion.229, bf16[4,64,64,256]{3,2,1,0:T(8,128)(2,1)} %get-tuple-element.510, bf16[4,256,64,8]{1,3,2,0:T(8,128)(2,1)S(1)} %get-tuple-element.509, ...), kind=kOutput, calls=%fused_computation.37.clone.1 | convolution fusion | flops 56758528 | bytes 11931136 | tf_op jit(solution)/shard_map/while/body/eval_jaxpr/hij,ihe->jhe/dot_general | solution.py:120
  181.0 6.9 %bitcast_dynamic-update-slice_fusion.8 = bf16[4,64,64,256]{3,2,1,0:T(8,128)(2,1)} fusion(bf16[4,64,64,256]{3,2,1,0:T(8,128)(2,1)} %get-tuple-element.485, s32[]{:T(128)S(6)} %copy.99, bf16[4,64,64,256]{3,2,1,0:T(8,128)(2,1)} %get-tuple-element.510, f32[64,64,256]{2,1,0:T(8,128)} %fusion.229, bf16[4,256,64,8]{1,3,2,0:T(8,128)(2,1)S(1)} %get-tuple-element.509, ...), kind=kOutput, calls=%fused_computation.30.clone.1 | convolution fusion | flops 39850240 | bytes 13371904 | tf_op jit(solution)/shard_map/while/body/eval_jaxpr/sub | solution.py:114
  189.9 5.2 fusion.229
  195.0 6.8 %fusion.230 = bf16[4,64,64,8]{1,3,2,0:T(8,128)(2,1)} fusion(bf16[4,64,64,8]{1,3,2,0:T(8,128)(2,1)} %get-tuple-element.486, s32[]{:T(128)S(6)} %copy.99, bf16[4,256,64,8]{1,3,2,0:T(8,128)(2,1)S(1)} %get-tuple-element.505, f32[64,64,256]{2,1,0:T(8,128)} %fusion.229, bf16[4,64,64,256]{3,2,1,0:T(8,128)(2,1)} %get-tuple-element.510, ...), kind=kOutput, calls=%fused_computation.41.clone.1 | convolution fusion | flops 56692992 | bytes 11668992 | tf_op jit(solution)/shard_map/while/body/eval_jaxpr/hij,jhe->ihe/dot_general | solution.py:117
  205.2 7.0 %fusion.231 = f32[4,256,64,8]{1,3,2,0:T(8,128)} fusion(f32[4,256,64,8]{1,3,2,0:T(8,128)} %get-tuple-element.487, s32[]{:T(128)S(6)} %copy.99, f32[64,64,256]{2,1,0:T(8,128)} %fusion.229, bf16[4,64,64,256]{3,2,1,0:T(8,128)(2,1)} %get-tuple-element.510, bf16[4,256,64,8]{1,3,2,0:T(8,128)(2,1)S(1)} %get-tuple-element.509, ...), kind=kOutput, calls=%fused_computation.37.clone.1 | convolution fusion | flops 56758528 | bytes 11931136 | tf_op jit(solution)/shard_map/while/body/eval_jaxpr/hij,ihe->jhe/dot_general | solution.py:120
  212.1 6.9 %bitcast_dynamic-update-slice_fusion.8 = bf16[4,64,64,256]{3,2,1,0:T(8,128)(2,1)} fusion(bf16[4,64,64,256]{3,2,1,0:T(8,128)(2,1)} %get-tuple-element.485, s32[]{:T(128)S(6)} %copy.99, bf16[4,64,64,256]{3,2,1,0:T(8,128)(2,1)} %get-tuple-element.510, f32[64,64,256]{2,1,0:T(8,128)} %fusion.229, bf16[4,256,64,8]{1,3,2,0:T(8,128)(2,1)S(1)} %get-tuple-element.509, ...), kind=kOutput, calls=%fused_computation.30.clone.1 | convolution fusion | flops 39850240 | bytes 13371904 | tf_op jit(solution)/shard_map/while/body/eval_jaxpr/sub | solution.py:114
  221.0 5.2 fusion.229
  226.1 6.8 %fusion.230 = bf16[4,64,64,8]{1,3,2,0:T(8,128)(2,1)} fusion(bf16[4,64,64,8]{1,3,2,0:T(8,128)(2,1)} %get-tuple-element.486, s32[]{:T(128)S(6)} %copy.99, bf16[4,256,64,8]{1,3,2,0:T(8,128)(2,1)S(1)} %get-tuple-element.505, f32[64,64,256]{2,1,0:T(8,128)} %fusion.229, bf16[4,64,64,256]{3,2,1,0:T(8,128)(2,1)} %get-tuple-element.510, ...), kind=kOutput, calls=%fused_computation.41.clone.1 | convolution fusion | flops 56692992 | bytes 11668992 | tf_op jit(solution)/shard_map/while/body/eval_jaxpr/hij,jhe->ihe/dot_general | solution.py:117
  236.3 7.0 %fusion.231 = f32[4,256,64,8]{1,3,2,0:T(8,128)} fusion(f32[4,256,64,8]{1,3,2,0:T(8,128)} %get-tuple-element.487, s32[]{:T(128)S(6)} %copy.99, f32[64,64,256]{2,1,0:T(8,128)} %fusion.229, bf16[4,64,64,256]{3,2,1,0:T(8,128)(2,1)} %get-tuple-element.510, bf16[4,256,64,8]{1,3,2,0:T(8,128)(2,1)S(1)} %get-tuple-element.509, ...), kind=kOutput, calls=%fused_computation.37.clone.1 | convolution fusion | flops 56758528 | bytes 11931136 | tf_op jit(solution)/shard_map/while/body/eval_jaxpr/hij,ihe->jhe/dot_general | solution.py:120
  243.3 6.9 %bitcast_dynamic-update-slice_fusion.8 = bf16[4,64,64,256]{3,2,1,0:T(8,128)(2,1)} fusion(bf16[4,64,64,256]{3,2,1,0:T(8,128)(2,1)} %get-tuple-element.485, s32[]{:T(128)S(6)} %copy.99, bf16[4,64,64,256]{3,2,1,0:T(8,128)(2,1)} %get-tuple-element.510, f32[64,64,256]{2,1,0:T(8,128)} %fusion.229, bf16[4,256,64,8]{1,3,2,0:T(8,128)(2,1)S(1)} %get-tuple-element.509, ...), kind=kOutput, calls=%fused_computation.30.clone.1 | convolution fusion | flops 39850240 | bytes 13371904 | tf_op jit(solution)/shard_map/while/body/eval_jaxpr/sub | solution.py:114
  261.0 37.3 %reduce-scatter.11.cloned.1.call-done = f32[4,64,512]{2,1,0:T(8,128)} async-done(((f32[4,256,512]{2,1,0:T(8,128)}), f32[4,64,512]{2,1,0:T(8,128)}) %reduce-scatter.11.cloned.1.call-update) | async-done | bytes 524304 | tf_op jit(solution)/shard_map/reduce_scatter | solution.py:233
  300.8 43.2 %reduce-scatter.9.cloned.1.call-done = f32[4,64,512]{2,1,0:T(8,128)} async-done(((f32[4,256,512]{2,1,0:T(8,128)}), f32[4,64,512]{2,1,0:T(8,128)}) %reduce-scatter.9.cloned.1.call-update) | async-done | bytes 524304 | tf_op jit(solution)/shard_map/reduce_scatter | solution.py:227
  361.4 21.0 %reduce-scatter.19.cloned.1.call-done = f32[64,512]{1,0:T(8,128)} async-done(((f32[512,512]{1,0:T(8,128)}), f32[64,512]{1,0:T(8,128)}) %reduce-scatter.19.cloned.1.call-update) | async-done | bytes 131088 | tf_op jit(solution)/shard_map/reduce_scatter | solution.py:283
  383.9 37.5 %reduce-scatter.13.cloned.1.call-done = f32[64,512]{1,0:T(8,128)} async-done(((f32[512,512]{1,0:T(8,128)}), f32[64,512]{1,0:T(8,128)}) %reduce-scatter.13.cloned.1.call-update) | async-done | bytes 131088 | tf_op jit(solution)/shard_map/reduce_scatter | solution.py:278
  424.1 36.4 %reduce-scatter.17.cloned.1.call-done = f32[64,512]{1,0:T(8,128)} async-done(((f32[512,512]{1,0:T(8,128)}), f32[64,512]{1,0:T(8,128)}) %reduce-scatter.17.cloned.1.call-update) | async-done | bytes 131088 | tf_op jit(solution)/shard_map/reduce_scatter | solution.py:281
  462.1 37.7 %reduce-scatter.15.cloned.1.call-done = f32[64,512]{1,0:T(8,128)} async-done(((f32[512,512]{1,0:T(8,128)}), f32[64,512]{1,0:T(8,128)}) %reduce-scatter.15.cloned.1.call-update) | async-done | bytes 131088 | tf_op jit(solution)/shard_map/reduce_scatter | solution.py:280
  501.3 53.1 %reduce-scatter.23.cloned.1.call-done = f32[256,512]{1,0:T(8,128)} async-done(((f32[2048,512]{1,0:T(8,128)}), f32[256,512]{1,0:T(8,128)}) %reduce-scatter.23.cloned.1.call-update) | async-done | bytes 524304 | tf_op jit(solution)/shard_map/reduce_scatter | solution.py:289
  556.2 53.3 %reduce-scatter.21.cloned.1.call-done = f32[64,2048]{1,0:T(8,128)} async-done(((f32[512,2048]{1,0:T(8,128)}), f32[64,2048]{1,0:T(8,128)}) %reduce-scatter.21.cloned.1.call-update) | async-done | bytes 524304 | tf_op jit(solution)/shard_map/reduce_scatter | solution.py:287
  613.9 24.0 %all-reduce.9 = (bf16[512]{0:T(512)(128)(2,1)S(1)}, bf16[512]{0:T(512)(128)(2,1)S(1)}, bf16[512]{0:T(512)(128)(2,1)S(1)}, bf16[512]{0:T(512)(128)(2,1)S(1)}, bf1...) all-reduce(f32[512]{0:T(512)S(1)} %get-tuple-element.213, ...), channel_id=4, replica_groups=mesh['batch'=8,'rows'=4] {'batch'}, use_global_device_ids=true, to_apply=%region_18.19.clone | all-reduce | flops 6144 | bytes 36864
  638.6 12.2 %all-reduce.10 = (bf16[64]{0:T(256)(128)(2,1)S(1)}, bf16[64]{0:T(256)(128)(2,1)S(1)}, bf16[64]{0:T(256)(128)(2,1)S(1)}, bf16[64]{0:T(256)(128)(2,1)S(1)}, bf16[6...) all-reduce(bf16[64]{0:T(256)(128)(2,1)S(1)} %dynamic-slice.35, ...), channel_id=1, replica_groups=mesh['batch'=8,'rows'=4] {'rows'}, use_global_device_ids=true, to_apply=%region_19.20 | all-reduce | flops 768 | bytes 3072 | tf_op jit(solution)/shard_map/psum | solution.py:309
  (263 shorter events, 176.4 us)
Async XLA Ops:
  7.2 105.1 %copy-start = (bf16[512,2048]{1,0:T(8,128)(2,1)S(1)}, bf16[512,2048]{1,0:T(8,128)(2,1)}, u32[]{:S(2)}) copy-start(bf16[512,2048]{1,0:T(8,128)(2,1)} %param.38) | copy-start | bytes 6291460
  7.2 14.1 %copy-start.39 = (bf16[512]{0:T(512)(128)(2,1)S(1)}, bf16[512]{0:T(512)(128)(2,1)}, u32[]{:S(2)}) copy-start(bf16[512]{0:T(512)(128)(2,1)} %param.36) | copy-start | bytes 3076
  7.2 14.1 %copy-start.40 = (bf16[512]{0:T(512)(128)(2,1)S(1)}, bf16[512]{0:T(512)(128)(2,1)}, u32[]{:S(2)}) copy-start(bf16[512]{0:T(512)(128)(2,1)} %param.37) | copy-start | bytes 3076
  7.3 48.5 %all-gather.2.cloned.1.call-start = ((), (), s32[]{:S(2)}) async-start(), calls=%async_computation.8 | async-start | bytes 1310720 | tf_op jit(solution)/shard_map/all_gather | solution.py:166
  14.4 34.3 %collective-permute-start.2 = (bf16[4,64,512]{2,1,0:T(8,128)(2,1)S(1)}, bf16[4,64,512]{2,1,0:T(8,128)(2,1)}, u32[]{:S(2)}, u32[]{:S(2)}) collective-permute-start(bf16[4,64,512]{2,1,0:T(8,128)(2,1)S(1)} %fusion.125), channel_id=1, source_target_pairs={{0,3},{1,0},{2,1},{3,2},{4,7},{5,4},{6,5},{7,6},{8,11},{9,8},{10,9... | collective-permute-start | bytes 786440 | tf_op jit(solution)/shard_map/ppermute | solution.py:24
  19.5 12.2 %collective-permute-start = (bf16[4,64,512]{2,1,0:T(8,128)(2,1)S(1)}, bf16[4,64,512]{2,1,0:T(8,128)(2,1)}, u32[]{:S(2)}, u32[]{:S(2)}) collective-permute-start(bf16[4,64,512]{2,1,0:T(8,128)(2,1)S(1)} %fusion.125), channel_id=1, source_target_pairs={{0,1},{1,2},{2,3},{3,0},{4,5},{5,6},{6,7},{7,4},{8,9},{9,10},{10,1... | collective-permute-start | bytes 786440 | tf_op jit(solution)/shard_map/ppermute | solution.py:21
  20.5 13.7 %copy-start.12 = (bf16[4,64,512]{2,1,0:T(8,128)(2,1)S(1)}, bf16[4,64,512]{2,1,0:T(8,128)(2,1)}, u32[]{:S(2)}) copy-start(bf16[4,64,512]{2,1,0:T(8,128)(2,1)} %param.42) | copy-start | bytes 786436
  20.5 277.7 %reduce-scatter.11.cloned.1.call-start = ((), (), s32[]{:S(2)}) async-start(), calls=%async_computation.10 | async-start | bytes 2621440 | tf_op jit(solution)/shard_map/reduce_scatter | solution.py:233
  31.7 16.0 %collective-permute-start.1 = (bf16[4,64,512]{2,1,0:T(8,128)(2,1)}, bf16[4,64,512]{2,1,0:T(8,128)(2,1)S(1)}, u32[]{:S(2)}, u32[]{:S(2)}) collective-permute-start(bf16[4,64,512]{2,1,0:T(8,128)(2,1)} %collective-permute-done), channel_id=1, source_target_pairs={{0,1},{1,2},{2,3},{3,0},{4,5},{5,6},{6,7},{7,4},{8,9},{9,10},{10,1... | collective-permute-start | bytes 786440 | tf_op jit(solution)/shard_map/ppermute | solution.py:21
  119.4 136.9 %copy-start.8 = (f32[256,512]{1,0:T(8,128)}, f32[256,512]{1,0:T(8,128)S(1)}, u32[]{:S(2)}) copy-start(f32[256,512]{1,0:T(8,128)S(1)} %get-tuple-element.290) | copy-start | bytes 1572868
  253.2 90.8 %reduce-scatter.9.cloned.1.call-start = ((), (), s32[]{:S(2)}) async-start(), calls=%async_computation.9 | async-start | bytes 2621440 | tf_op jit(solution)/shard_map/reduce_scatter | solution.py:227
  256.2 126.2 %reduce-scatter.19.cloned.1.call-start = ((), (), s32[]{:S(2)}) async-start(), calls=%async_computation.14 | async-start | bytes 1179648 | tf_op jit(solution)/shard_map/reduce_scatter | solution.py:283
  258.4 163.0 %reduce-scatter.13.cloned.1.call-start = ((), (), s32[]{:S(2)}) async-start(), calls=%async_computation.11 | async-start | bytes 1179648 | tf_op jit(solution)/shard_map/reduce_scatter | solution.py:278
  259.5 41.2 %copy-start.16 = (bf16[256,512]{0,1:T(8,128)(2,1)}, bf16[256,512]{0,1:T(8,128)(2,1)S(1)}, u32[]{:S(2)}) copy-start(bf16[256,512]{0,1:T(8,128)(2,1)S(1)} %reshape.266) | copy-start | bytes 786436
  260.9 199.6 %reduce-scatter.17.cloned.1.call-start = ((), (), s32[]{:S(2)}) async-start(), calls=%async_computation.13 | async-start | bytes 1179648 | tf_op jit(solution)/shard_map/reduce_scatter | solution.py:281
  300.7 46.4 %copy-start.10 = (f32[256,2048]{1,0:T(8,128)S(1)}, f32[256,2048]{1,0:T(8,128)}, u32[]{:S(2)}) copy-start(f32[256,2048]{1,0:T(8,128)} %get-tuple-element.297) | copy-start | bytes 6291460
  300.7 46.5 %copy-start.14 = (bf16[4,64,512]{2,1,0:T(8,128)(2,1)S(1)}, bf16[4,64,512]{2,1,0:T(8,128)(2,1)}, u32[]{:S(2)}) copy-start(bf16[4,64,512]{2,1,0:T(8,128)(2,1)} %param.42) | copy-start | bytes 786436
  300.7 199.0 %reduce-scatter.15.cloned.1.call-start = ((), (), s32[]{:S(2)}) async-start(), calls=%async_computation.12 | async-start | bytes 1179648 | tf_op jit(solution)/shard_map/reduce_scatter | solution.py:280
  347.1 207.3 %reduce-scatter.23.cloned.1.call-start = ((), (), s32[]{:S(2)}) async-start(), calls=%async_computation.16 | async-start | bytes 4718592 | tf_op jit(solution)/shard_map/reduce_scatter | solution.py:289
  350.1 259.4 %reduce-scatter.21.cloned.1.call-start = ((), (), s32[]{:S(2)}) async-start(), calls=%async_computation.15 | async-start | bytes 4718592 | tf_op jit(solution)/shard_map/reduce_scatter | solution.py:287
  354.3 305.1 %all-reduce.14.cloned.1.call-start = ((), (), s32[]{:S(2)}) async-start(), calls=%async_computation.17 | async-start | bytes 1572864 | tf_op jit(solution)/shard_map/psum | solution.py:311
  357.5 65.5 %copy-start.19 = (bf16[4,64,512]{2,1,0:T(8,128)(2,1)S(1)}, bf16[4,64,512]{2,1,0:T(8,128)(2,1)}, u32[]{:S(2)}) copy-start(bf16[4,64,512]{2,1,0:T(8,128)(2,1)} %copy-done.18) | copy-start | bytes 786436
  357.5 65.4 %copy-start.21 = (bf16[512,512]{1,0:T(8,128)(2,1)S(1)}, bf16[512,512]{1,0:T(8,128)(2,1)}, u32[]{:S(2)}) copy-start(bf16[512,512]{1,0:T(8,128)(2,1)} %param.31) | copy-start | bytes 1572868
  423.0 188.3 %copy-start.28 = (bf16[4,64,512]{2,1,0:T(8,128)(2,1)S(1)}, bf16[4,64,512]{2,1,0:T(8,128)(2,1)}, u32[]{:S(2)}) copy-start(bf16[4,64,512]{2,1,0:T(8,128)(2,1)} %copy-done.27) | copy-start | bytes 786436
  423.0 188.3 %copy-start.32 = (f32[256]{0:T(256)S(1)}, f32[256]{0:T(256)}, u32[]{:S(2)}) copy-start(f32[256]{0:T(256)} %copy-done.31) | copy-start | bytes 3076
  423.0 188.3 %copy-start.34 = (f32[256]{0:T(256)S(1)}, f32[256]{0:T(256)}, u32[]{:S(2)}) copy-start(f32[256]{0:T(256)} %copy-done.33) | copy-start | bytes 3076
  556.2 57.7 %copy-start.35 = (f32[512]{0:T(512)S(1)}, f32[512]{0:T(512)}, u32[]{:S(2)}) copy-start(f32[512]{0:T(512)} %get-tuple-element.289) | copy-start | bytes 6148
  556.2 57.7 %copy-start.36 = (f32[2048]{0:T(1024)S(1)}, f32[2048]{0:T(1024)}, u32[]{:S(2)}) copy-start(f32[2048]{0:T(1024)} %get-tuple-element.287) | copy-start | bytes 24580
  556.2 57.7 %copy-start.37 = (f32[512]{0:T(512)S(1)}, f32[512]{0:T(512)}, u32[]{:S(2)}) copy-start(f32[512]{0:T(512)} %get-tuple-element.211) | copy-start | bytes 6148
  556.2 57.7 %copy-start.38 = (f32[512]{0:T(512)S(1)}, f32[512]{0:T(512)}, u32[]{:S(2)}) copy-start(f32[512]{0:T(512)} %get-tuple-element.217) | copy-start | bytes 6148
  556.2 99.3 %copy-start.9 = (f32[256,512]{1,0:T(8,128)S(1)}, f32[256,512]{1,0:T(8,128)}, u32[]{:S(2)}) copy-start(f32[256,512]{1,0:T(8,128)} %copy-done.8) | copy-start | bytes 1572868
  611.3 57.7 %copy-start.1 = (bf16[512,2048]{1,0:T(8,128)(2,1)S(1)}, bf16[512,2048]{1,0:T(8,128)(2,1)}, u32[]{:S(2)}) copy-start(bf16[512,2048]{1,0:T(8,128)(2,1)} %param.38) | copy-start | bytes 6291460
  (24 other events, 77.9 us)
Sparse Core Ops, SparseCore 0:
  20.7 35.0 all-gather.1
  253.3 44.9 reduce-scatter.10
  300.7 43.2 reduce-scatter.8
  347.0 35.3 reduce-scatter.18
  385.4 35.9 reduce-scatter.12
  424.4 36.0 reduce-scatter.16
  463.7 35.9 reduce-scatter.14
  503.1 51.2 reduce-scatter.22
  558.1 51.3 reduce-scatter.20
  613.3 46.0 all-reduce.13
